TPU v7x, 32 devices: a whole 2x2x4 slice. The times are simulated.
32 devices in a mesh: sec: 8 (over y, x, core), img: 4 (over z).
Axes of the slice: x: 2, y: 2, z: 4, core: 2. Of those that a mesh axis runs over, the one named last changes fastest.
Arguments:
- saved_last: bfloat16 [8, 4, 4, 21, 21, 384], P('sec', None, 'img'), may hold values from -6 to 6
- saved_older: bfloat16 [8, 4, 4, 21, 21, 384], P('sec', None, 'img'), may hold values from -6 to 6
- arriving: bfloat16 [8, 2, 4, 21, 21, 384], P('sec', None, 'img'), may hold values from -6 to 6
- head_adjoint: bfloat16 [3, 2, 4, 21, 21, 384], P(None, None, 'img'), may hold values from -6 to 6
- plan: int32 [8, 4], P('sec'), may hold values from 0 to 3, each once within a row
- depth_five: bfloat16 [8, 25, 384], P('sec'), may hold values from -1.25 to 1.25
- depth_three: bfloat16 [8, 9, 384], P('sec'), may hold values from -2 to 2
- point_five: bfloat16 [8, 384, 384], P('sec'), may hold values from -0.3125 to 0.3125
- point_three: bfloat16 [8, 384, 384], P('sec'), may hold values from -0.3125 to 0.3125
Outputs:
- outgoing: bfloat16 [8, 2, 4, 21, 21, 384], P('sec', None, 'img')
- grad_point_five: float32 [8, 384, 384], P('sec', 'img')
- grad_depth_five: float32 [8, 384, 25], P('sec', 'img')
- grad_point_three: float32 [8, 384, 384], P('sec', 'img')
- grad_depth_three: float32 [8, 384, 9], P('sec', 'img')
Inputs may be any that keep to these rules, and one draw needn't show every extreme that they name: `plan`: each row is a permutation of the stash slots.
All inputs are finite; a program needn't handle non-finite values.
Results may differ from a plain program's by a relative error of at most 0.012.
Values may be sent and summed in bfloat16 or wider, within the bound.
A program may use at most 128 MiB of HBM per device.

v0:
```python
import functools

import jax
import jax.numpy as jnp
from jax import lax
from jax.experimental import pallas as pl
from jax.experimental.pallas import tpu as pltpu
from jax.sharding import PartitionSpec as P

F32 = jnp.float32
BF16 = jnp.bfloat16
LANES = 128
ROWS = 3
MESH = pl.DeviceIdType.MESH


def up(value, unit):
    return -(-value // unit) * unit


def spread(ref, tap, lanes, height):
    return jnp.broadcast_to(ref[tap : tap + 1, lanes], (height, LANES))


def turned(block, shift, height):
    shift = shift % height
    return block if shift == 0 else pltpu.roll(block, shift, 0)


def filtered(source, taps, kernel, first, lanes, breadth, back):
    radius = kernel // 2
    held = [source[first + k, :, lanes] for k in range(ROWS + kernel - 1)]
    totals = [None] * ROWS
    for col_tap in range(kernel):
        parts = [None] * ROWS
        for row_tap in range(kernel):
            tap = spread(taps, row_tap * kernel + col_tap, lanes, breadth)
            for row in range(ROWS):
                at = row + (kernel - 1 - row_tap if back else row_tap)
                term = tap * held[at]
                parts[row] = term if parts[row] is None else parts[row] + term
        shift = col_tap - radius if back else radius - col_tap
        for row in range(ROWS):
            moved = turned(parts[row], shift, breadth)
            totals[row] = moved if totals[row] is None else totals[row] + moved
    return totals


def tap_sums(active, back, sums, kernel, first, lanes, breadth):
    radius = kernel // 2
    held = [active[first + k, :, lanes] for k in range(ROWS + kernel - 1)]
    rows = [back[first + radius + row, :, lanes] for row in range(ROWS)]
    for col_tap in range(kernel):
        moved = [turned(row, col_tap - radius, breadth) for row in rows]
        for row_tap in range(kernel):
            total = None
            for row in range(ROWS):
                term = held[row + row_tap] * moved[row]
                total = term if total is None else total + term
            folded = total[0:8]
            for part in range(8, breadth, 8):
                folded = folded + total[part : part + 8]
            tap = row_tap * kernel + col_tap
            sums[tap, :, lanes] = sums[tap, :, lanes] + folded


def kernel_body(
    sections,
    group,
    kernels,
    plan,
    last,
    older,
    arriving,
    head,
    depth_five,
    depth_three,
    point_five,
    point_three,
    outgoing,
    out_five,
    out_three,
    out_taps,
    inbox,
    outbox,
    active_five,
    active_three,
    back_five,
    back_three,
    grad_wide,
    grad_flat,
    mixed,
    taps_five,
    taps_three,
    total_five,
    total_three,
    sums_five,
    sums_three,
    sums_all,
    give_five,
    give_three,
    take_five,
    take_three,
    local_sem,
    send_sem,
    recv_sem,
    give_sem,
    take_sem,
):
    five, three = kernels
    turns, height, width, channels = last.shape
    breadth = grad_wide.shape[1]
    rows = channels // group
    factor = 1.0 / (height * width)
    blocks = channels // LANES
    groups = height // ROWS
    sec = lax.axis_index("sec")
    img = lax.axis_index("img")
    top = sec == sections - 1
    bottom = sec == 0
    not_top = sec < sections - 1
    not_bottom = sec > 0

    def first_copy(which):
        return pltpu.make_async_copy(arriving.at[which], inbox.at[0, which], local_sem.at[0, which])

    def head_copy(turn, which):
        return pltpu.make_async_copy(
            head.at[turn - 1, which], inbox.at[turn, which], local_sem.at[turn, which]
        )

    for which in range(2):
        first_copy(which).start()

    @pl.when(top)
    def _():
        for turn in range(1, turns):
            for which in range(2):
                head_copy(turn, which).start()

    barrier = pltpu.get_barrier_semaphore()
    for step in range(1, group):
        pl.semaphore_signal(
            barrier,
            inc=1,
            device_id={"sec": sec, "img": lax.rem(img + step, group)},
            device_id_type=MESH,
        )

    @pl.when(not_bottom)
    def _():
        pl.semaphore_signal(
            barrier, inc=1, device_id={"sec": sec - 1, "img": img}, device_id_type=MESH
        )

    @pl.when(not_top)
    def _():
        pl.semaphore_signal(
            barrier, inc=1, device_id={"sec": sec + 1, "img": img}, device_id_type=MESH
        )

    for ref in (active_five, active_three, back_five, back_three, sums_five, sums_three):
        ref[...] = jnp.zeros(ref.shape, ref.dtype)
    for ref in (total_five, total_three, sums_all, grad_wide):
        ref[...] = jnp.zeros(ref.shape, ref.dtype)
    taps_five[...] = depth_five[...].astype(F32)
    taps_three[...] = depth_three[...].astype(F32)

    def prepare(turn):
        slot = plan[0, turn]

        def one(row, carry):
            active_five[row + five // 2, 0:width, :] = jnp.maximum(last[slot, row].astype(F32), 0.0)
            active_three[row + three // 2, 0:width, :] = jnp.maximum(
                older[slot, row].astype(F32), 0.0
            )
            return carry

        lax.fori_loop(0, height, one, 0)

    def hop(turn, which):
        return pltpu.make_async_remote_copy(
            src_ref=outbox.at[turn, which],
            dst_ref=inbox.at[turn + 1, which],
            send_sem=send_sem.at[turn, which],
            recv_sem=recv_sem.at[turn, which],
            device_id={"sec": lax.max(sec - 1, 0), "img": img},
            device_id_type=MESH,
        )

    def arrive(turn, which):
        @pl.when(top)
        def _():
            head_copy(turn, which).wait()

        @pl.when(not_top)
        def _():
            hop(turn - 1, which).wait_recv()

    def spread_grad(turn):
        def one(row, carry):
            grad_wide[row, 0:width, :] = inbox[turn, 0, row].astype(F32)
            return carry

        lax.fori_loop(0, height, one, 0)
        grad_flat[...] = grad_wide[...].reshape(height * breadth, channels).astype(BF16)

    def pull(weights, back, kernel):
        product = lax.dot_general(
            grad_flat[...], weights[...], (((1,), (1,)), ((), ())), preferred_element_type=F32
        )
        back[kernel // 2 : kernel // 2 + height] = product.reshape(height, breadth, channels)

    def each_block(work):
        def one(index, carry):
            lanes = pl.ds(pl.multiple_of((index // groups) * LANES, LANES), LANES)
            work((index % groups) * ROWS, lanes)
            return carry

        lax.fori_loop(0, blocks * groups, one, 0)

    def through_five(turn, target):
        def work(first, lanes):
            outs = filtered(back_five, taps_five, five, first, lanes, breadth, True)
            for row in range(ROWS):
                at = first + row
                kept = jnp.where(active_five[at + five // 2, :, lanes] > 0, outs[row], 0.0)
                extra = inbox[turn, 1, at, :, lanes].astype(F32)
                done = kept[0:width] + grad_wide[at, 0:width, lanes] + extra
                target[at, :, lanes] = done.astype(BF16)

        each_block(work)

    def through_three(target):
        def work(first, lanes):
            outs = filtered(back_three, taps_three, three, first, lanes, breadth, True)
            for row in range(ROWS):
                at = first + row
                kept = jnp.where(active_three[at + three // 2, :, lanes] > 0, outs[row], 0.0)
                target[at, :, lanes] = kept[0:width].astype(BF16)

        each_block(work)

    def weights(active, taps, back, sums, total, kernel):
        def work(first, lanes):
            outs = filtered(active, taps, kernel, first, lanes, breadth, False)
            for row in range(ROWS):
                mixed[first + row, :, lanes] = outs[row]
            tap_sums(active, back, sums, kernel, first, lanes, breadth)

        each_block(work)
        flat = mixed[...].reshape(height * breadth, channels).astype(BF16)
        total[...] += lax.dot_general(
            flat, grad_flat[...], (((0,), (0,)), ((), ())), preferred_element_type=F32
        )

    def weights_five():
        weights(active_five, taps_five, back_five, sums_five, total_five, five)

    def weights_three():
        weights(active_three, taps_three, back_three, sums_three, total_three, three)

    def share(part, step):
        source, target = ((give_five, take_five), (give_three, take_three))[part]
        peer = lax.rem(img + step, group)
        return pltpu.make_async_remote_copy(
            src_ref=source.at[peer],
            dst_ref=target.at[step],
            send_sem=give_sem.at[part, step],
            recv_sem=take_sem.at[part, step],
            device_id={"sec": sec, "img": peer},
            device_id_type=MESH,
        )

    prepare(0)
    callers = group + 1 - bottom.astype(jnp.int32) - top.astype(jnp.int32)
    pl.semaphore_wait(barrier, callers)

    first_copy(0).wait()
    first_copy(1).wait()

    def turn_work(turn, carry):
        spread_grad(turn)
        pull(point_five, back_five, five)

        @pl.when(turn > 0)
        def _():
            arrive(turn, 1)

        through_five(turn, outbox.at[turn, 0])

        @pl.when(not_bottom)
        def _():
            hop(turn, 0).start()

        pull(point_three, back_three, three)
        through_three(outbox.at[turn, 1])

        @pl.when(not_bottom)
        def _():
            hop(turn, 1).start()

        weights_five()
        weights_three()
        prepare(turn + 1)
        arrive(turn + 1, 0)
        return carry

    lax.fori_loop(0, turns - 1, turn_work, 0)

    end = turns - 1
    spread_grad(end)
    pull(point_five, back_five, five)
    pull(point_three, back_three, three)
    weights_five()
    for peer in range(group):
        give_five[peer] = (total_five[peer * rows : (peer + 1) * rows] * factor).astype(BF16)
    for step in range(1, group):
        share(0, step).start()
    weights_three()
    count_five, count_three = five * five, three * three
    sums_all[0:count_five] = jnp.sum(sums_five[...], axis=1)
    sums_all[count_five : count_five + count_three] = jnp.sum(sums_three[...], axis=1)
    flipped = sums_all[...].T * factor
    for peer in range(group):
        part = slice(peer * rows, (peer + 1) * rows)
        give_three[peer, :, 0:channels] = (total_three[part] * factor).astype(BF16)
        give_three[peer, :, channels:] = flipped[part].astype(BF16)
    for step in range(1, group):
        share(1, step).start()
    arrive(end, 1)
    through_five(end, outgoing.at[0])
    through_three(outgoing.at[1])

    gathered_five = give_five[img].astype(F32)
    for step in range(1, group):
        share(0, step).wait_recv()
        gathered_five = gathered_five + take_five[step].astype(F32)
    out_five[...] = gathered_five
    gathered = give_three[img].astype(F32)
    for step in range(1, group):
        share(1, step).wait_recv()
        gathered = gathered + take_three[step].astype(F32)
    out_three[...] = gathered[:, 0:channels]
    out_taps[...] = gathered[:, channels:]
    for part in range(2):
        for step in range(1, group):
            share(part, step).wait_send()

    @pl.when(not_bottom)
    def _():
        for turn in range(turns - 1):
            for which in range(2):
                hop(turn, which).wait_send()


def local(
    sections,
    group,
    saved_last,
    saved_older,
    arriving,
    head_adjoint,
    plan,
    depth_five,
    depth_three,
    point_five,
    point_three,
):
    turns, _, height, width, channels = saved_last.shape[1:]
    count_five, count_three = depth_five.shape[1], depth_three.shape[1]
    five, three = round(count_five**0.5), round(count_three**0.5)
    breadth = up(width + five // 2, 8)
    rows = channels // group
    vmem = pl.BlockSpec(memory_space=pltpu.VMEM)
    smem = pl.BlockSpec(memory_space=pltpu.SMEM)
    outside = pl.BlockSpec(memory_space=pl.ANY)
    body = functools.partial(kernel_body, sections, group, (five, three))
    outgoing, grad_five, grad_three, grad_taps = pl.pallas_call(
        body,
        out_shape=(
            jax.ShapeDtypeStruct((2, height, width, channels), BF16),
            jax.ShapeDtypeStruct((rows, channels), F32),
            jax.ShapeDtypeStruct((rows, channels), F32),
            jax.ShapeDtypeStruct((rows, LANES), F32),
        ),
        in_specs=[smem, vmem, vmem, outside, outside, vmem, vmem, vmem, vmem],
        out_specs=(vmem, vmem, vmem, vmem),
        scratch_shapes=[
            pltpu.VMEM((turns, 2, height, width, channels), BF16),
            pltpu.VMEM((turns - 1, 2, height, width, channels), BF16),
            pltpu.VMEM((height + five - 1, breadth, channels), F32),
            pltpu.VMEM((height + three - 1, breadth, channels), F32),
            pltpu.VMEM((height + five - 1, breadth, channels), F32),
            pltpu.VMEM((height + three - 1, breadth, channels), F32),
            pltpu.VMEM((height, breadth, channels), F32),
            pltpu.VMEM((height * breadth, channels), BF16),
            pltpu.VMEM((height, breadth, channels), F32),
            pltpu.VMEM((count_five, channels), F32),
            pltpu.VMEM((count_three, channels), F32),
            pltpu.VMEM((channels, channels), F32),
            pltpu.VMEM((channels, channels), F32),
            pltpu.VMEM((count_five, 8, channels), F32),
            pltpu.VMEM((count_three, 8, channels), F32),
            pltpu.VMEM((LANES, channels), F32),
            pltpu.VMEM((group, rows, channels), BF16),
            pltpu.VMEM((group, rows, channels + LANES), BF16),
            pltpu.VMEM((group, rows, channels), BF16),
            pltpu.VMEM((group, rows, channels + LANES), BF16),
            pltpu.SemaphoreType.DMA((turns, 2)),
            pltpu.SemaphoreType.DMA((turns - 1, 2)),
            pltpu.SemaphoreType.DMA((turns - 1, 2)),
            pltpu.SemaphoreType.DMA((2, group)),
            pltpu.SemaphoreType.DMA((2, group)),
        ],
        compiler_params=pltpu.CompilerParams(collective_id=0, has_side_effects=True),
    )(
        plan,
        saved_last.reshape(turns, height, width, channels),
        saved_older.reshape(turns, height, width, channels),
        arriving.reshape(2, height, width, channels),
        head_adjoint.reshape(turns - 1, 2, height, width, channels),
        depth_five[0],
        depth_three[0],
        point_five[0],
        point_three[0],
    )
    return (
        outgoing.reshape(1, 2, 1, height, width, channels),
        grad_five[None],
        grad_taps[None, :, :count_five],
        grad_three[None],
        grad_taps[None, :, count_five : count_five + count_three],
    )


def solution(mesh):
    placed = (
        P("sec", None, "img", None, None, None),
        P("sec", None, "img", None, None, None),
        P("sec", None, "img", None, None, None),
        P(None, None, "img", None, None, None),
        P("sec", None),
        P("sec", None, None),
        P("sec", None, None),
        P("sec", None, None),
        P("sec", None, None),
    )
    return jax.shard_map(
        functools.partial(local, mesh.shape["sec"], mesh.shape["img"]),
        mesh=mesh,
        in_specs=placed,
        out_specs=(
            P("sec", None, "img", None, None, None),
            P("sec", "img", None),
            P("sec", "img", None),
            P("sec", "img", None),
            P("sec", "img", None),
        ),
        check_vma=False,
    )
```

profile of v0, /device:TPU:1, one launch (start us, length us, event | category | flops | bytes accessed | tf_op | source)
XLA Modules:
  0.0 72.3 jit_solution(2757557841114150399)
XLA Ops:
  0.6 2.1 %copy.26 = bf16[1,2,1,21,21,384]{5,4,3,1,2,0:T(8,128)(2,1)} copy(bf16[1,2,1,21,21,384]{5,1,4,3,2,0:T(2,128)(2,1)} %param.11) | data formatting | bytes 1354752 | tf_op args[2]
  2.8 0.0 copy-start
  2.8 0.0 copy-start.1
  2.8 3.5 %copy.25 = bf16[3,2,1,21,21,384]{5,4,3,1,0,2:T(8,128)(2,1)} copy(bf16[3,2,1,21,21,384]{5,1,4,3,2,0:T(2,128)(2,1)} %param.12) | data formatting | bytes 4064256 | tf_op args[3]
  6.2 0.0 copy-done
  6.2 0.0 copy-done.1
  6.2 2.1 %copy_bitcast_fusion.1 = (bf16[4,21,21,384]{3,2,1,0:T(8,128)(2,1)}, bf16[4,21,21,384]{3,2,1,0:T(8,128)(2,1)}) fusion(bf16[1,4,1,21,21,384]{5,1,4,3,2,0:T(4,128)(2,1)S(1)} %copy-done, bf16[1,4,1,21,21,384]{5,1,4,3,2,0:T(4,128)(2,1)S(1)} %copy-done.1), kind=kLoop, calls=%fused_computation.1 | loop fusion | bytes 5419008 | tf_op jit(solution)/shard_map/reshape | solution.py:420
  8.3 57.8 %shard_map.128 = (bf16[2,21,21,384]{3,2,1,0:T(8,128)(2,1)}, f32[96,384]{1,0:T(8,128)}, f32[96,384]{1,0:T(8,128)}, f32[96,128]{1,0:T(8,128)}) custom-call(s32[1,4]{1,0:T(1,128)} %plan.1, bf16[4,21,21,384]{3,2,1,0:T(8,128)(2,1)} %get-tuple-element.19.last, bf16[4,21,21,384]{3,2,1,0:T(8,128)(2,1)} %get-tuple-element.18.older, ...), custom_call_target="tpu_custom_call" | custom-call | tf_op jit(solution)/shard_map/pallas_call | solution.py:379
  66.2 0.0 copy-start.2
  66.2 0.0 copy-start.4
  66.2 0.0 copy-start.3
  66.2 2.5 %copy.18 = bf16[1,2,1,21,21,384]{5,1,4,3,2,0:T(2,128)(2,1)} copy(bf16[1,2,1,21,21,384]{5,4,3,1,2,0:T(8,128)(2,1)} %bitcast.23) | data formatting | bytes 1354752
  68.7 0.9 %slice_bitcast_fusion = f32[1,96,9]{2,1,0:T(8,128)S(1)} fusion(f32[96,128]{1,0:T(8,128)} %get-tuple-element.11), kind=kLoop, calls=%fused_computation.4 | loop fusion | bytes 6912 | tf_op jit(solution)/shard_map/broadcast_in_dim | solution.py:433
  69.6 0.7 copy.20
  70.3 0.0 copy-done.2
  70.3 0.7 copy.19
  71.0 0.0 copy-done.4
  71.0 0.7 copy.29
  71.6 0.0 copy-done.3
  71.6 0.7 copy.30
  (1 shorter events, 0.0 us)
Async XLA Ops:
  2.8 3.5 %copy-start = (bf16[1,4,1,21,21,384]{5,1,4,3,2,0:T(4,128)(2,1)S(1)}, bf16[1,4,1,21,21,384]{5,1,4,3,2,0:T(4,128)(2,1)}, u32[]{:S(2)}) copy-start(bf16[1,4,1,21,21,384]{5,1,4,3,2,0:T(4,128)(2,1)} %param.10) | copy-start | bytes 4064260
  2.8 3.5 %copy-start.1 = (bf16[1,4,1,21,21,384]{5,1,4,3,2,0:T(4,128)(2,1)S(1)}, bf16[1,4,1,21,21,384]{5,1,4,3,2,0:T(4,128)(2,1)}, u32[]{:S(2)}) copy-start(bf16[1,4,1,21,21,384]{5,1,4,3,2,0:T(4,128)(2,1)} %param.9) | copy-start | bytes 4064260
  66.2 4.1 %copy-start.2 = (f32[96,128]{1,0:T(8,128)S(1)}, f32[96,128]{1,0:T(8,128)}, u32[]{:S(2)}) copy-start(f32[96,128]{1,0:T(8,128)} %get-tuple-element.11) | copy-start | bytes 147460
  66.2 4.8 %copy-start.4 = (f32[96,384]{1,0:T(8,128)S(1)}, f32[96,384]{1,0:T(8,128)}, u32[]{:S(2)}) copy-start(f32[96,384]{1,0:T(8,128)} %get-tuple-element.10) | copy-start | bytes 442372
  66.2 5.5 %copy-start.3 = (f32[96,384]{1,0:T(8,128)S(1)}, f32[96,384]{1,0:T(8,128)}, u32[]{:S(2)}) copy-start(f32[96,384]{1,0:T(8,128)} %get-tuple-element.12) | copy-start | bytes 442372
where the time goes:
time: 72.6 us; the launch traced here: 72.3 us
  Pallas kernels  57.8 us (80%)
  local copies, waits for them, and re-layouts  13.8 us (19%)
    pallas_call x1, Pallas kernels, local(): pl.pallas_call(body, out_shape=(jax.ShapeDtypeStruct((2, height, width, c...  57.8 us
    unnamed x17, local copies, waits for them, and re-layouts  10.8 us
    reshape x1, local copies, waits for them, and re-layouts, local(): saved_older.reshape(turns, height, width, channels)  2.1 us

commit v1 on v0

v1 whole, which is shorter than its diff:
```python
import functools

import jax
import jax.numpy as jnp
from jax import lax
from jax.experimental import pallas as pl
from jax.experimental.pallas import tpu as pltpu
from jax.sharding import PartitionSpec as P

F32 = jnp.float32
BF16 = jnp.bfloat16
LANES = 128
WIDE = 256
MESH = pl.DeviceIdType.MESH


def up(value, unit):
    return -(-value // unit) * unit


def turned(block, shift):
    shift = shift % block.shape[0]
    return block if shift == 0 else pltpu.roll(block, shift, 0)


def rows_at(even, odd, pair, offset, lanes):
    if offset % 2 == 0:
        block = even[pair + offset // 2 + 1, :, lanes]
    else:
        block = odd[pair + (offset + 1) // 2, :, lanes]
    return block.reshape(-1, 8, WIDE)


def filtered(even, odd, taps, kernel, pair, lanes, back):
    radius = kernel // 2
    held = [rows_at(even, odd, pair, k - radius, lanes) for k in range(kernel)]
    total = None
    for col_tap in range(kernel):
        part = None
        for row_tap in range(kernel):
            at = kernel - 1 - row_tap if back else row_tap
            term = taps[row_tap * kernel + col_tap, :, lanes][None] * held[at]
            part = term if part is None else part + term
        wide = part.astype(F32).reshape(-1, WIDE)
        moved = turned(wide, col_tap - radius if back else radius - col_tap)
        total = moved if total is None else total + moved
    return total


def tap_sums(even, odd, back, sums, kernel, pair, lanes):
    radius = kernel // 2
    held = [rows_at(even, odd, pair, k - radius, lanes) for k in range(kernel)]
    wide = back[pair + 1, :, lanes].astype(F32)
    for col_tap in range(kernel):
        moved = turned(wide, col_tap - radius).astype(BF16).reshape(-1, 8, WIDE)
        for row_tap in range(kernel):
            term = held[row_tap] * moved
            folded = term[0]
            for part in range(1, term.shape[0]):
                folded = folded + term[part]
            tap = row_tap * kernel + col_tap
            sums[tap, :, lanes] = sums[tap, :, lanes] + folded.astype(F32)


def kernel_body(
    sections,
    group,
    kernels,
    plan,
    last,
    older,
    arriving,
    head,
    depth_five,
    depth_three,
    point_five,
    point_three,
    outgoing,
    out_five,
    out_three,
    out_taps,
    inbox,
    outbox,
    stage,
    even_last,
    odd_last,
    even_older,
    odd_older,
    even_five,
    odd_five,
    even_three,
    odd_three,
    grad_wide,
    grad_flat,
    mixed,
    taps_five,
    taps_three,
    total_five,
    total_three,
    sums_five,
    sums_three,
    sums_all,
    give_five,
    give_three,
    take_five,
    take_three,
    local_sem,
    send_sem,
    recv_sem,
    give_sem,
    take_sem,
):
    five, three = kernels
    turns, height, width, channels = last.shape
    breadth = grad_wide.shape[1]
    rows = channels // group
    factor = 1.0 / (height * width)
    blocks = 2 * channels // WIDE
    columns = channels // LANES
    pairs = grad_wide.shape[0] // 2
    sec = lax.axis_index("sec")
    img = lax.axis_index("img")
    top = sec == sections - 1
    bottom = sec == 0
    not_top = sec < sections - 1
    not_bottom = sec > 0

    def first_copy(which):
        return pltpu.make_async_copy(arriving.at[which], inbox.at[0, which, pl.ds(0, height)], local_sem.at[0, which])

    def head_copy(turn, which):
        return pltpu.make_async_copy(
            head.at[turn - 1, which], inbox.at[turn, which, pl.ds(0, height)], local_sem.at[turn, which]
        )

    for which in range(2):
        first_copy(which).start()

    @pl.when(top)
    def _():
        for turn in range(1, turns):
            for which in range(2):
                head_copy(turn, which).start()

    barrier = pltpu.get_barrier_semaphore()
    for step in range(1, group):
        pl.semaphore_signal(
            barrier,
            inc=1,
            device_id={"sec": sec, "img": lax.rem(img + step, group)},
            device_id_type=MESH,
        )

    @pl.when(not_bottom)
    def _():
        pl.semaphore_signal(
            barrier, inc=1, device_id={"sec": sec - 1, "img": img}, device_id_type=MESH
        )

    @pl.when(not_top)
    def _():
        pl.semaphore_signal(
            barrier, inc=1, device_id={"sec": sec + 1, "img": img}, device_id_type=MESH
        )

    for ref in (sums_five, sums_three, total_five, total_three, sums_all):
        ref[...] = jnp.zeros(ref.shape, ref.dtype)
    edge_even = jnp.zeros(even_five.shape[1:], BF16)
    for ref in (even_last, even_older, even_five, even_three):
        ref[0] = edge_even
        ref[pairs + 1] = edge_even
    for ref in (odd_last, odd_older, odd_five, odd_three):
        ref[pairs] = edge_even
    for row in range(stage.shape[0]):
        stage[row, breadth - 8 : breadth] = jnp.zeros((8, channels), F32)
    for row in range(grad_wide.shape[0]):
        grad_wide[row, breadth - 8 : breadth] = jnp.zeros((8, channels), F32)
    for row in (0, *range(height + 1, stage.shape[0])):
        stage[row] = jnp.zeros((breadth, channels), F32)
    for row in range(height, grad_wide.shape[0]):
        grad_wide[row] = jnp.zeros((breadth, channels), F32)
    for wide, packed in ((depth_five, taps_five), (depth_three, taps_three)):
        for tap in range(packed.shape[0]):
            value = jnp.broadcast_to(wide[tap : tap + 1].astype(F32), (8, channels))
            packed[tap] = jnp.concatenate([value, value], 1).astype(BF16)

    def prepare(turn):
        slot = plan[0, turn]
        for saved, even, odd in ((last, even_last, odd_last), (older, even_older, odd_older)):

            def one(row, carry):
                stage[row + 1, 0:width, :] = jnp.maximum(saved[slot, row].astype(F32), 0.0)
                return carry

            lax.fori_loop(0, height, one, 0, unroll=3)

            def two(pair, carry):
                rows = [stage[2 * pair + k] for k in range(3)]
                odd[pair] = jnp.concatenate(rows[0:2], 1).astype(BF16)
                even[pair + 1] = jnp.concatenate(rows[1:3], 1).astype(BF16)
                return carry

            lax.fori_loop(0, pairs, two, 0)

    def hop(turn, which):
        return pltpu.make_async_remote_copy(
            src_ref=outbox.at[turn, which, pl.ds(0, height)],
            dst_ref=inbox.at[turn + 1, which, pl.ds(0, height)],
            send_sem=send_sem.at[turn, which],
            recv_sem=recv_sem.at[turn, which],
            device_id={"sec": lax.max(sec - 1, 0), "img": img},
            device_id_type=MESH,
        )

    def arrive(turn, which):
        @pl.when(top)
        def _():
            head_copy(turn, which).wait()

        @pl.when(not_top)
        def _():
            hop(turn - 1, which).wait_recv()

    def spread_grad(turn):
        def one(row, carry):
            grad_wide[row, 0:width, :] = inbox[turn, 0, row].astype(F32)
            return carry

        lax.fori_loop(0, height, one, 0, unroll=3)
        grad_flat[...] = grad_wide[0:height].reshape(-1, channels).astype(BF16)

    def pull(weights, even, odd):
        product = lax.dot_general(
            grad_flat[...], weights[...], (((1,), (1,)), ((), ())), preferred_element_type=F32
        )
        zeros = jnp.zeros((breadth, channels), F32)

        def line(row):
            inside = 0 <= row < height
            return product[row * breadth : (row + 1) * breadth] if inside else zeros

        for pair in range(pairs):
            even[pair + 1] = jnp.concatenate([line(2 * pair), line(2 * pair + 1)], 1).astype(BF16)
            odd[pair] = jnp.concatenate([line(2 * pair - 1), line(2 * pair)], 1).astype(BF16)

    def parts(pair, block):
        for part in range(WIDE // LANES):
            at = block * (WIDE // LANES) + part
            lanes = slice((at % columns) * LANES, (at % columns + 1) * LANES)
            yield 2 * pair + at // columns, lanes, slice(part * LANES, (part + 1) * LANES)

    def each_block(work):
        def one(pair, carry):
            for block in range(blocks):
                work(pair, block, slice(block * WIDE, (block + 1) * WIDE))
            return carry

        lax.fori_loop(0, pairs, one, 0)

    def through_five(turn, target):
        def work(pair, block, wide):
            out = filtered(even_five, odd_five, taps_five, five, pair, wide, True)
            kept = jnp.where(even_last[pair + 1, :, wide].astype(F32) > 0, out, 0.0)
            for at, lanes, cut in parts(pair, block):
                extra = inbox[turn, 1, at, :, lanes].astype(F32)
                done = kept[0:width, cut] + grad_wide[at, 0:width, lanes] + extra
                target[at, :, lanes] = done.astype(BF16)

        each_block(work)

    def through_three(target):
        def work(pair, block, wide):
            out = filtered(even_three, odd_three, taps_three, three, pair, wide, True)
            kept = jnp.where(even_older[pair + 1, :, wide].astype(F32) > 0, out, 0.0)
            for at, lanes, cut in parts(pair, block):
                target[at, :, lanes] = kept[0:width, cut].astype(BF16)

        each_block(work)

    def weights(even, odd, taps, back, sums, total, kernel):
        def work(pair, block, wide):
            out = filtered(even, odd, taps, kernel, pair, wide, False)
            for at, lanes, cut in parts(pair, block):
                mixed[at, :, lanes] = out[:, cut]
            tap_sums(even, odd, back, sums, kernel, pair, wide)

        each_block(work)
        flat = mixed[0:height].reshape(-1, channels).astype(BF16)
        total[...] += lax.dot_general(
            flat, grad_flat[...], (((0,), (0,)), ((), ())), preferred_element_type=F32
        )

    def weights_five():
        weights(even_last, odd_last, taps_five, even_five, sums_five, total_five, five)

    def weights_three():
        weights(even_older, odd_older, taps_three, even_three, sums_three, total_three, three)

    def share(part, step):
        source, target = ((give_five, take_five), (give_three, take_three))[part]
        peer = lax.rem(img + step, group)
        return pltpu.make_async_remote_copy(
            src_ref=source.at[peer],
            dst_ref=target.at[step],
            send_sem=give_sem.at[part, step],
            recv_sem=take_sem.at[part, step],
            device_id={"sec": sec, "img": peer},
            device_id_type=MESH,
        )

    prepare(0)
    callers = group + 1 - bottom.astype(jnp.int32) - top.astype(jnp.int32)
    pl.semaphore_wait(barrier, callers)

    first_copy(0).wait()
    first_copy(1).wait()

    def turn_work(turn, carry):
        spread_grad(turn)
        pull(point_five, even_five, odd_five)

        @pl.when(turn > 0)
        def _():
            arrive(turn, 1)

        through_five(turn, outbox.at[turn, 0])

        @pl.when(not_bottom)
        def _():
            hop(turn, 0).start()

        pull(point_three, even_three, odd_three)
        through_three(outbox.at[turn, 1])

        @pl.when(not_bottom)
        def _():
            hop(turn, 1).start()

        weights_five()
        weights_three()
        prepare(turn + 1)
        arrive(turn + 1, 0)
        return carry

    lax.fori_loop(0, turns - 1, turn_work, 0)

    end = turns - 1
    spread_grad(end)
    pull(point_five, even_five, odd_five)
    pull(point_three, even_three, odd_three)
    weights_five()
    for peer in range(group):
        give_five[peer] = (total_five[peer * rows : (peer + 1) * rows] * factor).astype(BF16)
    for step in range(1, group):
        share(0, step).start()
    weights_three()
    count_five, count_three = five * five, three * three
    for sums, start, count in ((sums_five, 0, count_five), (sums_three, count_five, count_three)):
        folded = jnp.sum(sums[...], axis=1)
        sums_all[start : start + count] = folded[:, 0:channels] + folded[:, channels:]
    flipped = sums_all[...].T * factor
    for peer in range(group):
        part = slice(peer * rows, (peer + 1) * rows)
        give_three[peer, :, 0:channels] = (total_three[part] * factor).astype(BF16)
        give_three[peer, :, channels:] = flipped[part].astype(BF16)
    for step in range(1, group):
        share(1, step).start()
    arrive(end, 1)
    through_five(end, outgoing.at[0])
    through_three(outgoing.at[1])

    gathered_five = give_five[img].astype(F32)
    for step in range(1, group):
        share(0, step).wait_recv()
        gathered_five = gathered_five + take_five[step].astype(F32)
    out_five[...] = gathered_five
    gathered = give_three[img].astype(F32)
    for step in range(1, group):
        share(1, step).wait_recv()
        gathered = gathered + take_three[step].astype(F32)
    out_three[...] = gathered[:, 0:channels]
    out_taps[...] = gathered[:, channels:]
    for part in range(2):
        for step in range(1, group):
            share(part, step).wait_send()

    @pl.when(not_bottom)
    def _():
        for turn in range(turns - 1):
            for which in range(2):
                hop(turn, which).wait_send()


def local(
    sections,
    group,
    saved_last,
    saved_older,
    arriving,
    head_adjoint,
    plan,
    depth_five,
    depth_three,
    point_five,
    point_three,
):
    turns, _, height, width, channels = saved_last.shape[1:]
    count_five, count_three = depth_five.shape[1], depth_three.shape[1]
    five, three = round(count_five**0.5), round(count_three**0.5)
    breadth = up(width + five // 2, 8)
    pairs = up(height, 2) // 2
    even = pltpu.VMEM((pairs + 2, breadth, 2 * channels), BF16)
    odd = pltpu.VMEM((pairs + 1, breadth, 2 * channels), BF16)
    rows = channels // group
    vmem = pl.BlockSpec(memory_space=pltpu.VMEM)
    smem = pl.BlockSpec(memory_space=pltpu.SMEM)
    outside = pl.BlockSpec(memory_space=pl.ANY)
    body = functools.partial(kernel_body, sections, group, (five, three))
    outgoing, grad_five, grad_three, grad_taps = pl.pallas_call(
        body,
        out_shape=(
            jax.ShapeDtypeStruct((2, 2 * pairs, width, channels), BF16),
            jax.ShapeDtypeStruct((rows, channels), F32),
            jax.ShapeDtypeStruct((rows, channels), F32),
            jax.ShapeDtypeStruct((rows, LANES), F32),
        ),
        in_specs=[smem, vmem, vmem, outside, outside, vmem, vmem, vmem, vmem],
        out_specs=(vmem, vmem, vmem, vmem),
        scratch_shapes=[
            pltpu.VMEM((turns, 2, 2 * pairs, width, channels), BF16),
            pltpu.VMEM((turns - 1, 2, 2 * pairs, width, channels), BF16),
            pltpu.VMEM((2 * pairs + 2, breadth, channels), F32),
            *([even, odd] * 4),
            pltpu.VMEM((2 * pairs, breadth, channels), F32),
            pltpu.VMEM((height * breadth, channels), BF16),
            pltpu.VMEM((2 * pairs, breadth, channels), F32),
            pltpu.VMEM((count_five, 8, 2 * channels), BF16),
            pltpu.VMEM((count_three, 8, 2 * channels), BF16),
            pltpu.VMEM((channels, channels), F32),
            pltpu.VMEM((channels, channels), F32),
            pltpu.VMEM((count_five, 8, 2 * channels), F32),
            pltpu.VMEM((count_three, 8, 2 * channels), F32),
            pltpu.VMEM((LANES, channels), F32),
            pltpu.VMEM((group, rows, channels), BF16),
            pltpu.VMEM((group, rows, channels + LANES), BF16),
            pltpu.VMEM((group, rows, channels), BF16),
            pltpu.VMEM((group, rows, channels + LANES), BF16),
            pltpu.SemaphoreType.DMA((turns, 2)),
            pltpu.SemaphoreType.DMA((turns - 1, 2)),
            pltpu.SemaphoreType.DMA((turns - 1, 2)),
            pltpu.SemaphoreType.DMA((2, group)),
            pltpu.SemaphoreType.DMA((2, group)),
        ],
        compiler_params=pltpu.CompilerParams(collective_id=0, has_side_effects=True),
    )(
        plan,
        saved_last.reshape(turns, height, width, channels),
        saved_older.reshape(turns, height, width, channels),
        arriving.reshape(2, height, width, channels),
        head_adjoint.reshape(turns - 1, 2, height, width, channels),
        depth_five[0],
        depth_three[0],
        point_five[0],
        point_three[0],
    )
    return (
        outgoing[:, :height].reshape(1, 2, 1, height, width, channels),
        grad_five[None],
        grad_taps[None, :, :count_five],
        grad_three[None],
        grad_taps[None, :, count_five : count_five + count_three],
    )


def solution(mesh):
    placed = (
        P("sec", None, "img", None, None, None),
        P("sec", None, "img", None, None, None),
        P("sec", None, "img", None, None, None),
        P(None, None, "img", None, None, None),
        P("sec", None),
        P("sec", None, None),
        P("sec", None, None),
        P("sec", None, None),
        P("sec", None, None),
    )
    return jax.shard_map(
        functools.partial(local, mesh.shape["sec"], mesh.shape["img"]),
        mesh=mesh,
        in_specs=placed,
        out_specs=(
            P("sec", None, "img", None, None, None),
            P("sec", "img", None),
            P("sec", "img", None),
            P("sec", "img", None),
            P("sec", "img", None),
        ),
        check_vma=False,
    )
```

time: 72.6 us -> 65.2 us (0.90)
  Pallas kernels: 57.8 us -> 51.3 us
  local copies, waits for them, and re-layouts: 13.8 us -> 13 us
    pallas_call x1, Pallas kernels: 57.8 us -> 51.3 us  [local(): pl.pallas_call(body, out_shape=(jax.ShapeDtypeStruct((2, 2 * pairs, width...]
    reshape x0 -> x1, local copies, waits for them, and re-layouts: none -> 1.26 us  [local(): outgoing[:, :height].reshape(1, 2, 1, height, width, channels)]
    unnamed x17, local copies, waits for them, and re-layouts: 10.8 us -> 9.61 us
    broadcast_in_dim x1, local copies, waits for them, and re-layouts: 0.87 us -> 0.07 us  [local(): grad_taps[None, :, count_five:count_five + count_three]]
where the time goes in v1:
time: 65.2 us; the launch traced here: 65 us
  Pallas kernels  51.3 us (79%)
  local copies, waits for them, and re-layouts  13 us (20%)
  between operations  0.67 us (1%)
    pallas_call x1, Pallas kernels, local(): pl.pallas_call(body, out_shape=(jax.ShapeDtypeStruct((2, 2 * pairs, width...  51.3 us
    unnamed x17, local copies, waits for them, and re-layouts  9.61 us
    reshape x1, local copies, waits for them, and re-layouts, local(): saved_older.reshape(turns, height, width, channels)  2.1 us

profile of v1, /device:TPU:1, one launch (start us, length us, event | category | flops | bytes accessed | tf_op | source)
XLA Modules:
  0.0 65.0 jit_solution(14111618335964710898)
XLA Ops:
  0.6 2.1 %copy.26 = bf16[1,2,1,21,21,384]{5,4,3,1,2,0:T(8,128)(2,1)} copy(bf16[1,2,1,21,21,384]{5,1,4,3,2,0:T(2,128)(2,1)} %param.11) | data formatting | bytes 1354752 | tf_op args[2]
  2.7 0.0 copy-start
  2.7 0.0 copy-start.1
  2.7 3.5 %copy.25 = bf16[3,2,1,21,21,384]{5,4,3,1,0,2:T(8,128)(2,1)} copy(bf16[3,2,1,21,21,384]{5,1,4,3,2,0:T(2,128)(2,1)} %param.12) | data formatting | bytes 4064256 | tf_op args[3]
  6.2 0.0 copy-done
  6.2 0.0 copy-done.1
  6.2 2.1 %copy_bitcast_fusion.1 = (bf16[4,21,21,384]{3,2,1,0:T(8,128)(2,1)}, bf16[4,21,21,384]{3,2,1,0:T(8,128)(2,1)}) fusion(bf16[1,4,1,21,21,384]{5,1,4,3,2,0:T(4,128)(2,1)S(1)} %copy-done, bf16[1,4,1,21,21,384]{5,1,4,3,2,0:T(4,128)(2,1)S(1)} %copy-done.1), kind=kLoop, calls=%fused_computation.1 | loop fusion | bytes 5419008 | tf_op jit(solution)/shard_map/reshape | solution.py:458
  8.3 51.3 %shard_map.128 = (bf16[2,22,21,384]{3,2,1,0:T(8,128)(2,1)}, f32[96,384]{1,0:T(8,128)}, f32[96,384]{1,0:T(8,128)}, f32[96,128]{1,0:T(8,128)}) custom-call(s32[1,4]{1,0:T(1,128)} %plan.1, bf16[4,21,21,384]{3,2,1,0:T(8,128)(2,1)} %get-tuple-element.19.last, bf16[4,21,21,384]{3,2,1,0:T(8,128)(2,1)} %get-tuple-element.18.older, ...), custom_call_target="tpu_custom_call" | custom-call | tf_op jit(solution)/shard_map/pallas_call | solution.py:419
  59.6 0.0 copy-start.2
  59.6 0.0 copy-start.4
  59.6 0.0 copy-start.3
  59.6 1.3 %slice_bitcast_fusion = bf16[1,2,1,21,21,384]{5,4,3,1,2,0:T(8,128)(2,1)S(1)} fusion(bf16[2,22,21,384]{3,2,1,0:T(8,128)(2,1)} %get-tuple-element.9), kind=kLoop, calls=%fused_computation.4 | loop fusion | bytes 1354752 | tf_op jit(solution)/shard_map/reshape | solution.py:467
  60.9 1.4 %copy.18 = bf16[1,2,1,21,21,384]{5,1,4,3,2,0:T(2,128)(2,1)} copy(bf16[1,2,1,21,21,384]{5,4,3,1,2,0:T(8,128)(2,1)S(1)} %slice_bitcast_fusion) | data formatting | bytes 1354752
  62.3 0.0 copy-done.2
  62.3 0.1 slice_bitcast_fusion.1
  62.4 0.7 %copy.20 = f32[1,96,9]{1,0,2:T(1,128)} copy(f32[1,96,9]{2,1,0:T(8,128)S(1)} %slice_bitcast_fusion.1) | data formatting | bytes 6912
  63.0 0.7 %copy.19 = f32[1,96,25]{1,0,2:T(1,128)} copy(f32[1,96,25]{2,1,0:T(8,128)S(1)} %slice_bitcast_fusion.2) | data formatting | bytes 19200
  63.7 0.0 copy-done.4
  63.7 0.7 %copy.29 = f32[1,96,384]{2,1,0:T(8,128)} copy(f32[1,96,384]{2,1,0:T(8,128)S(1)} %bitcast.27) | data formatting | bytes 294912
  64.4 0.0 copy-done.3
  64.4 0.7 %copy.30 = f32[1,96,384]{2,1,0:T(8,128)} copy(f32[1,96,384]{2,1,0:T(8,128)S(1)} %bitcast.26) | data formatting | bytes 294912
  (1 shorter events, 0.0 us)
Async XLA Ops:
  2.7 3.5 %copy-start = (bf16[1,4,1,21,21,384]{5,1,4,3,2,0:T(4,128)(2,1)S(1)}, bf16[1,4,1,21,21,384]{5,1,4,3,2,0:T(4,128)(2,1)}, u32[]{:S(2)}) copy-start(bf16[1,4,1,21,21,384]{5,1,4,3,2,0:T(4,128)(2,1)} %param.10) | copy-start | bytes 4064260
  2.7 3.5 %copy-start.1 = (bf16[1,4,1,21,21,384]{5,1,4,3,2,0:T(4,128)(2,1)S(1)}, bf16[1,4,1,21,21,384]{5,1,4,3,2,0:T(4,128)(2,1)}, u32[]{:S(2)}) copy-start(bf16[1,4,1,21,21,384]{5,1,4,3,2,0:T(4,128)(2,1)} %param.9) | copy-start | bytes 4064260
  59.6 2.7 %copy-start.2 = (f32[96,128]{1,0:T(8,128)S(1)}, f32[96,128]{1,0:T(8,128)}, u32[]{:S(2)}) copy-start(f32[96,128]{1,0:T(8,128)} %get-tuple-element.11) | copy-start | bytes 147460
  59.6 4.1 %copy-start.4 = (f32[96,384]{1,0:T(8,128)S(1)}, f32[96,384]{1,0:T(8,128)}, u32[]{:S(2)}) copy-start(f32[96,384]{1,0:T(8,128)} %get-tuple-element.10) | copy-start | bytes 442372
  59.6 4.8 %copy-start.3 = (f32[96,384]{1,0:T(8,128)S(1)}, f32[96,384]{1,0:T(8,128)}, u32[]{:S(2)}) copy-start(f32[96,384]{1,0:T(8,128)} %get-tuple-element.12) | copy-start | bytes 442372

commit v2 on v1

--- a/solution.py
+++ b/solution.py
@@ -69,8 +69,10 @@
     plan,
     last,
     older,
-    arriving,
-    head,
+    arriving_last,
+    arriving_older,
+    head_last,
+    head_older,
     depth_five,
     depth_three,
     point_five,
@@ -78,7 +80,8 @@
     outgoing,
     out_five,
     out_three,
-    out_taps,
+    out_taps_five,
+    out_taps_three,
     inbox,
     outbox,
     stage,
@@ -92,7 +95,8 @@
     odd_three,
     grad_wide,
     grad_flat,
-    mixed,
+    mixed_five,
+    mixed_three,
     taps_five,
     taps_three,
     total_five,
@@ -102,8 +106,10 @@
     sums_all,
     give_five,
     give_three,
+    give_taps,
     take_five,
     take_three,
+    take_taps,
     local_sem,
     send_sem,
     recv_sem,
@@ -126,12 +132,14 @@
     not_bottom = sec > 0
 
     def first_copy(which):
-        return pltpu.make_async_copy(arriving.at[which], inbox.at[0, which, pl.ds(0, height)], local_sem.at[0, which])
+        source = (arriving_last, arriving_older)[which]
+        target = inbox.at[0, which, pl.ds(0, height)]
+        return pltpu.make_async_copy(source, target, local_sem.at[0, which])
 
     def head_copy(turn, which):
-        return pltpu.make_async_copy(
-            head.at[turn - 1, which], inbox.at[turn, which, pl.ds(0, height)], local_sem.at[turn, which]
-        )
+        source = (head_last, head_older)[which].at[turn - 1]
+        target = inbox.at[turn, which, pl.ds(0, height)]
+        return pltpu.make_async_copy(source, target, local_sem.at[turn, which])
 
     for which in range(2):
         first_copy(which).start()
@@ -277,27 +285,34 @@
 
         each_block(work)
 
-    def weights(even, odd, taps, back, sums, total, kernel):
+    def forward():
         def work(pair, block, wide):
-            out = filtered(even, odd, taps, kernel, pair, wide, False)
-            for at, lanes, cut in parts(pair, block):
-                mixed[at, :, lanes] = out[:, cut]
-            tap_sums(even, odd, back, sums, kernel, pair, wide)
+            for even, odd, taps, mixed, kernel in (
+                (even_last, odd_last, taps_five, mixed_five, five),
+                (even_older, odd_older, taps_three, mixed_three, three),
+            ):
+                out = filtered(even, odd, taps, kernel, pair, wide, False)
+                for at, lanes, cut in parts(pair, block):
+                    mixed[at, :, lanes] = out[:, cut]
 
         each_block(work)
+
+    def add_taps():
+        def work(pair, block, wide):
+            tap_sums(even_last, odd_last, even_five, sums_five, five, pair, wide)
+            tap_sums(even_older, odd_older, even_three, sums_three, three, pair, wide)
+
+        each_block(work)
+
+    def add_point(mixed, total):
         flat = mixed[0:height].reshape(-1, channels).astype(BF16)
         total[...] += lax.dot_general(
             flat, grad_flat[...], (((0,), (0,)), ((), ())), preferred_element_type=F32
         )
 
-    def weights_five():
-        weights(even_last, odd_last, taps_five, even_five, sums_five, total_five, five)
-
-    def weights_three():
-        weights(even_older, odd_older, taps_three, even_three, sums_three, total_three, three)
-
     def share(part, step):
-        source, target = ((give_five, take_five), (give_three, take_three))[part]
+        source = (give_three, give_five, give_taps)[part]
+        target = (take_three, take_five, take_taps)[part]
         peer = lax.rem(img + step, group)
         return pltpu.make_async_remote_copy(
             src_ref=source.at[peer],
@@ -309,6 +324,7 @@
         )
 
     prepare(0)
+    forward()
     callers = group + 1 - bottom.astype(jnp.int32) - top.astype(jnp.int32)
     pl.semaphore_wait(barrier, callers)
 
@@ -336,9 +352,11 @@
         def _():
             hop(turn, 1).start()
 
-        weights_five()
-        weights_three()
+        add_point(mixed_five, total_five)
+        add_point(mixed_three, total_three)
+        add_taps()
         prepare(turn + 1)
+        forward()
         arrive(turn + 1, 0)
         return carry
 
@@ -346,41 +364,46 @@
 
     end = turns - 1
     spread_grad(end)
+    for part, mixed, total, give in (
+        (0, mixed_three, total_three, give_three),
+        (1, mixed_five, total_five, give_five),
+    ):
+        add_point(mixed, total)
+        for peer in range(group):
+            give[peer] = (total[peer * rows : (peer + 1) * rows] * factor).astype(BF16)
+        for step in range(1, group):
+            share(part, step).start()
     pull(point_five, even_five, odd_five)
     pull(point_three, even_three, odd_three)
-    weights_five()
-    for peer in range(group):
-        give_five[peer] = (total_five[peer * rows : (peer + 1) * rows] * factor).astype(BF16)
-    for step in range(1, group):
-        share(0, step).start()
-    weights_three()
+    add_taps()
     count_five, count_three = five * five, three * three
     for sums, start, count in ((sums_five, 0, count_five), (sums_three, count_five, count_three)):
         folded = jnp.sum(sums[...], axis=1)
         sums_all[start : start + count] = folded[:, 0:channels] + folded[:, channels:]
     flipped = sums_all[...].T * factor
     for peer in range(group):
-        part = slice(peer * rows, (peer + 1) * rows)
-        give_three[peer, :, 0:channels] = (total_three[part] * factor).astype(BF16)
-        give_three[peer, :, channels:] = flipped[part].astype(BF16)
+        give_taps[peer] = flipped[peer * rows : (peer + 1) * rows].astype(BF16)
     for step in range(1, group):
-        share(1, step).start()
+        share(2, step).start()
     arrive(end, 1)
     through_five(end, outgoing.at[0])
     through_three(outgoing.at[1])
 
-    gathered_five = give_five[img].astype(F32)
-    for step in range(1, group):
-        share(0, step).wait_recv()
-        gathered_five = gathered_five + take_five[step].astype(F32)
-    out_five[...] = gathered_five
-    gathered = give_three[img].astype(F32)
-    for step in range(1, group):
-        share(1, step).wait_recv()
-        gathered = gathered + take_three[step].astype(F32)
-    out_three[...] = gathered[:, 0:channels]
-    out_taps[...] = gathered[:, channels:]
-    for part in range(2):
+    def gathered(part, give, take):
+        value = give[img].astype(F32)
+        for step in range(1, group):
+            share(part, step).wait_recv()
+            value = value + take[step].astype(F32)
+        return value
+
+    out_three[...] = gathered(0, give_three, take_three)
+    out_five[...] = gathered(1, give_five, take_five)
+    by_tap = gathered(2, give_taps, take_taps).T
+    for tap in range(count_five):
+        out_taps_five[tap] = by_tap[tap : tap + 1]
+    for tap in range(count_three):
+        out_taps_three[tap] = by_tap[count_five + tap : count_five + tap + 1]
+    for part in range(3):
         for step in range(1, group):
             share(part, step).wait_send()
 
@@ -416,16 +439,17 @@
     smem = pl.BlockSpec(memory_space=pltpu.SMEM)
     outside = pl.BlockSpec(memory_space=pl.ANY)
     body = functools.partial(kernel_body, sections, group, (five, three))
-    outgoing, grad_five, grad_three, grad_taps = pl.pallas_call(
+    outgoing, grad_five, grad_three, taps_five, taps_three = pl.pallas_call(
         body,
         out_shape=(
             jax.ShapeDtypeStruct((2, 2 * pairs, width, channels), BF16),
             jax.ShapeDtypeStruct((rows, channels), F32),
             jax.ShapeDtypeStruct((rows, channels), F32),
-            jax.ShapeDtypeStruct((rows, LANES), F32),
+            jax.ShapeDtypeStruct((count_five, 1, rows), F32),
+            jax.ShapeDtypeStruct((count_three, 1, rows), F32),
         ),
-        in_specs=[smem, vmem, vmem, outside, outside, vmem, vmem, vmem, vmem],
-        out_specs=(vmem, vmem, vmem, vmem),
+        in_specs=[smem, vmem, vmem, *[outside] * 4, *[vmem] * 4],
+        out_specs=(vmem,) * 5,
         scratch_shapes=[
             pltpu.VMEM((turns, 2, 2 * pairs, width, channels), BF16),
             pltpu.VMEM((turns - 1, 2, 2 * pairs, width, channels), BF16),
@@ -433,6 +457,7 @@
             *([even, odd] * 4),
             pltpu.VMEM((2 * pairs, breadth, channels), F32),
             pltpu.VMEM((height * breadth, channels), BF16),
+            pltpu.VMEM((2 * pairs, breadth, channels), F32),
             pltpu.VMEM((2 * pairs, breadth, channels), F32),
             pltpu.VMEM((count_five, 8, 2 * channels), BF16),
             pltpu.VMEM((count_three, 8, 2 * channels), BF16),
@@ -442,22 +467,26 @@
             pltpu.VMEM((count_three, 8, 2 * channels), F32),
             pltpu.VMEM((LANES, channels), F32),
             pltpu.VMEM((group, rows, channels), BF16),
-            pltpu.VMEM((group, rows, channels + LANES), BF16),
             pltpu.VMEM((group, rows, channels), BF16),
-            pltpu.VMEM((group, rows, channels + LANES), BF16),
+            pltpu.VMEM((group, rows, LANES), BF16),
+            pltpu.VMEM((group, rows, channels), BF16),
+            pltpu.VMEM((group, rows, channels), BF16),
+            pltpu.VMEM((group, rows, LANES), BF16),
             pltpu.SemaphoreType.DMA((turns, 2)),
             pltpu.SemaphoreType.DMA((turns - 1, 2)),
             pltpu.SemaphoreType.DMA((turns - 1, 2)),
-            pltpu.SemaphoreType.DMA((2, group)),
-            pltpu.SemaphoreType.DMA((2, group)),
+            pltpu.SemaphoreType.DMA((3, group)),
+            pltpu.SemaphoreType.DMA((3, group)),
         ],
         compiler_params=pltpu.CompilerParams(collective_id=0, has_side_effects=True),
     )(
         plan,
         saved_last.reshape(turns, height, width, channels),
         saved_older.reshape(turns, height, width, channels),
-        arriving.reshape(2, height, width, channels),
-        head_adjoint.reshape(turns - 1, 2, height, width, channels),
+        arriving[0, 0, 0],
+        arriving[0, 1, 0],
+        head_adjoint[:, 0, 0],
+        head_adjoint[:, 1, 0],
         depth_five[0],
         depth_three[0],
         point_five[0],
@@ -466,9 +495,9 @@
     return (
         outgoing[:, :height].reshape(1, 2, 1, height, width, channels),
         grad_five[None],
-        grad_taps[None, :, :count_five],
+        taps_five.transpose(1, 2, 0),
         grad_three[None],
-        grad_taps[None, :, count_five : count_five + count_three],
+        taps_three.transpose(1, 2, 0),
     )
 
 

time: 65.2 us -> 68.2 us (1.046)
  local copies, waits for them, and re-layouts: 13 us -> 17.6 us
  Pallas kernels: 51.3 us -> 49.7 us
    slice x0 -> x2, local copies, waits for them, and re-layouts: none -> 6.6 us  [the longest x1 5.66 us: local(): head_adjoint[:, 1, 0]]
    unnamed x17 -> x19, local copies, waits for them, and re-layouts: 9.61 us -> 4.58 us
    squeeze x0 -> x2, local copies, waits for them, and re-layouts: none -> 3.07 us  [the longest x1 2.03 us: local(): head_adjoint[:, 1, 0]]
    pallas_call x1, Pallas kernels: 51.3 us -> 49.7 us  [local(): pl.pallas_call(body, out_shape=(jax.ShapeDtypeStruct((2, 2 * pairs, width...]
where the time goes in v2:
time: 68.2 us; the launch traced here: 68 us
  Pallas kernels  49.7 us (73%)
  local copies, waits for them, and re-layouts  17.6 us (26%)
  between operations  0.7 us (1%)
    pallas_call x1, Pallas kernels, local(): pl.pallas_call(body, out_shape=(jax.ShapeDtypeStruct((2, 2 * pairs, width...  49.7 us
    slice x1, local copies, waits for them, and re-layouts, local(): head_adjoint[:, 1, 0]  5.66 us
    unnamed x19, local copies, waits for them, and re-layouts  4.58 us
    reshape x1, local copies, waits for them, and re-layouts, local(): saved_older.reshape(turns, height, width, channels)  2.07 us
    squeeze x1, local copies, waits for them, and re-layouts, local(): head_adjoint[:, 1, 0]  2.03 us

profile of v2, /device:TPU:1, one launch (start us, length us, event | category | flops | bytes accessed | tf_op | source)
XLA Modules:
  0.0 68.0 jit_solution(13574996268241779472)
XLA Ops:
  0.6 5.7 %fusion = (bf16[3,1,1,21,21,384]{5,1,4,3,2,0:T(2,128)(2,1)S(1)}, bf16[3,1,1,21,21,384]{5,1,4,3,2,0:T(2,128)(2,1)S(1)}) fusion(bf16[3,2,1,21,21,384]{5,1,4,3,2,0:T(2,128)(2,1)} %param.12), kind=kLoop, calls=%fused_computation.7 | loop fusion | bytes 4064256 | tf_op jit(solution)/shard_map/slice | solution.py:489
  6.3 0.0 copy-start
  6.3 2.0 %copy_bitcast_fusion.2 = (bf16[3,21,21,384]{3,2,1,0:T(8,128)(2,1)}, bf16[3,21,21,384]{3,2,1,0:T(8,128)(2,1)}) fusion(bf16[3,1,1,21,21,384]{5,1,4,3,2,0:T(2,128)(2,1)S(1)} %get-tuple-element.20, bf16[3,1,1,21,21,384]{5,1,4,3,2,0:T(2,128)(2,1)S(1)} %get-tuple-element.21), kind=kLoop, calls=%fused_computation.2 | loop fusion | bytes 4064256 | tf_op jit(solution)/shard_map/squeeze | solution.py:489
  8.3 0.0 copy-done
  8.3 0.0 copy-start.2
  8.3 0.9 %fusion.1 = (bf16[1,1,1,21,21,384]{5,1,4,3,2,0:T(2,128)(2,1)S(1)}, bf16[1,1,1,21,21,384]{5,1,4,3,2,0:T(2,128)(2,1)S(1)}) fusion(bf16[1,2,1,21,21,384]{5,1,4,3,2,0:T(2,128)(2,1)S(1)} %copy-done), kind=kLoop, calls=%fused_computation.8 | loop fusion | bytes 1354752 | tf_op jit(solution)/shard_map/slice | solution.py:487
  9.3 0.0 copy-start.1
  9.3 1.0 %copy_bitcast_fusion.4 = (bf16[21,21,384]{2,1,0:T(8,128)(2,1)}, bf16[21,21,384]{2,1,0:T(8,128)(2,1)}) fusion(bf16[1,1,1,21,21,384]{5,1,4,3,2,0:T(2,128)(2,1)S(1)} %get-tuple-element.22, bf16[1,1,1,21,21,384]{5,1,4,3,2,0:T(2,128)(2,1)S(1)} %get-tuple-element.23), kind=kLoop, calls=%fused_computation.5 | loop fusion | bytes 1354752 | tf_op jit(solution)/shard_map/squeeze | solution.py:487
  10.3 0.0 copy-done.2
  10.3 0.7 copy-done.1
  11.0 2.1 %copy_bitcast_fusion = (bf16[4,21,21,384]{3,2,1,0:T(8,128)(2,1)}, bf16[4,21,21,384]{3,2,1,0:T(8,128)(2,1)}) fusion(bf16[1,4,1,21,21,384]{5,1,4,3,2,0:T(4,128)(2,1)S(1)} %copy-done.1, bf16[1,4,1,21,21,384]{5,1,4,3,2,0:T(4,128)(2,1)S(1)} %copy-done.2), kind=kLoop, calls=%fused_computation | loop fusion | bytes 5419008 | tf_op jit(solution)/shard_map/reshape | solution.py:485
  13.1 49.7 %shard_map.128 = (bf16[2,22,21,384]{3,2,1,0:T(8,128)(2,1)}, f32[96,384]{1,0:T(8,128)}, f32[96,384]{1,0:T(8,128)}, f32[25,1,96]{2,1,0:T(1,128)}, f32[9,1,96]{2,1,0:T(1,128)}) custom-call(s32[1,4]{1,0:T(1,128)} %plan.1, bf16[4,21,21,384]{3,2,1,0:T(8,128)(2,1)} %get-tuple-element.29.last, bf16[4,21,21,384]{3,2,1,0:T(8,128)(2,1)} %get-tuple-element.28.older, ...), custom_call_target="tpu_custom_call" | custom-call | tf_op jit(solution)/shard_map/pallas_call | solution.py:442
  62.8 0.0 copy-start.4
  62.8 0.0 copy-start.5
  62.8 0.0 copy-start.3
  62.8 0.0 copy-start.6
  62.8 1.3 %slice_bitcast_fusion = bf16[1,2,1,21,21,384]{5,4,3,1,2,0:T(8,128)(2,1)S(1)} fusion(bf16[2,22,21,384]{3,2,1,0:T(8,128)(2,1)} %get-tuple-element.10), kind=kLoop, calls=%fused_computation.4 | loop fusion | bytes 1354752 | tf_op jit(solution)/shard_map/reshape | solution.py:496
  64.1 1.4 %copy.20 = bf16[1,2,1,21,21,384]{5,1,4,3,2,0:T(2,128)(2,1)} copy(bf16[1,2,1,21,21,384]{5,4,3,1,2,0:T(8,128)(2,1)S(1)} %slice_bitcast_fusion) | data formatting | bytes 1354752
  65.5 0.0 copy-done.4
  65.5 0.7 copy.35
  66.1 0.0 copy-done.5
  66.1 0.6 copy.36
  66.7 0.0 copy-done.3
  66.7 0.7 copy.37
  67.4 0.0 copy-done.6
  67.4 0.6 copy.38
Async XLA Ops:
  6.3 2.0 %copy-start = (bf16[1,2,1,21,21,384]{5,1,4,3,2,0:T(2,128)(2,1)S(1)}, bf16[1,2,1,21,21,384]{5,1,4,3,2,0:T(2,128)(2,1)}, u32[]{:S(2)}) copy-start(bf16[1,2,1,21,21,384]{5,1,4,3,2,0:T(2,128)(2,1)} %param.11) | copy-start | bytes 2032132
  8.3 2.0 %copy-start.2 = (bf16[1,4,1,21,21,384]{5,1,4,3,2,0:T(4,128)(2,1)S(1)}, bf16[1,4,1,21,21,384]{5,1,4,3,2,0:T(4,128)(2,1)}, u32[]{:S(2)}) copy-start(bf16[1,4,1,21,21,384]{5,1,4,3,2,0:T(4,128)(2,1)} %param.9) | copy-start | bytes 4064260
  9.3 1.7 %copy-start.1 = (bf16[1,4,1,21,21,384]{5,1,4,3,2,0:T(4,128)(2,1)S(1)}, bf16[1,4,1,21,21,384]{5,1,4,3,2,0:T(4,128)(2,1)}, u32[]{:S(2)}) copy-start(bf16[1,4,1,21,21,384]{5,1,4,3,2,0:T(4,128)(2,1)} %param.10) | copy-start | bytes 4064260
  62.8 2.7 %copy-start.4 = (f32[96,384]{1,0:T(8,128)S(1)}, f32[96,384]{1,0:T(8,128)}, u32[]{:S(2)}) copy-start(f32[96,384]{1,0:T(8,128)} %get-tuple-element.11) | copy-start | bytes 442372
  62.8 3.4 %copy-start.5 = (f32[25,1,96]{2,1,0:T(1,128)S(1)}, f32[25,1,96]{2,1,0:T(1,128)}, u32[]{:S(2)}) copy-start(f32[25,1,96]{2,1,0:T(1,128)} %get-tuple-element.12) | copy-start | bytes 28804
  62.8 4.0 %copy-start.3 = (f32[96,384]{1,0:T(8,128)S(1)}, f32[96,384]{1,0:T(8,128)}, u32[]{:S(2)}) copy-start(f32[96,384]{1,0:T(8,128)} %get-tuple-element.13) | copy-start | bytes 442372
  62.8 4.6 %copy-start.6 = (f32[9,1,96]{2,1,0:T(1,128)S(1)}, f32[9,1,96]{2,1,0:T(1,128)}, u32[]{:S(2)}) copy-start(f32[9,1,96]{2,1,0:T(1,128)} %get-tuple-element.14) | copy-start | bytes 10372
